TPU v7x, 32 devices: a whole 2x2x4 slice. The times are simulated.
32 devices in a mesh: tm: 8 (over z, x), dp: 4 (over y, core).
Axes of the slice: x: 2, y: 2, z: 4, core: 2. Of those that a mesh axis runs over, the one named last changes fastest.
Arguments:
- frames: bfloat16 [4, 1024, 1024], P('dp', 'tm'), may hold values from -6 to 6
- grad_frames: bfloat16 [4, 1024, 1024], P('dp', 'tm'), may hold values from -6 to 6
- w_qkv: bfloat16 [1024, 2304], replicated, may hold values from -0.1875 to 0.1875
- w_out: bfloat16 [1024, 768], replicated, may hold values from -0.21875 to 0.21875
Outputs:
- grad_input: bfloat16 [4, 1024, 1024], P('dp', 'tm')
- grad_qkv: float32 [1024, 2304], P('tm')
- grad_out: float32 [1024, 768], P('tm')
All inputs are finite; a program needn't handle non-finite values.
Results may differ from a plain program's by a relative error of at most 0.014.
Values sent between devices are 32-bit elements; how exact they have to be, the bound alone decides.
A program may use at most 64 MiB of HBM per device.

v0:
```python
import jax
import jax.numpy as jnp
from jax import lax
from jax.sharding import PartitionSpec as P

HEADS = 12
HEAD = 64
BLOCK = 128


def prefix(value, axis, combine, identity, reverse):
    peers, here = (lax.axis_size(axis), lax.axis_index(axis))
    everything = jax.tree.map(lambda part: lax.all_gather(part, axis), value)
    start = jax.tree.map(
        lambda part, zero: jnp.broadcast_to(jnp.asarray(zero, part.dtype), part.shape),
        value,
        identity,
    )

    def step(k, before):
        at = peers - 1 - k if reverse else k
        reached = at > here if reverse else at < here
        new = combine(before, jax.tree.map(lambda part: part[at], everything))
        return jax.tree.map(lambda a, b: jnp.where(reached, a, b), new, before)

    return lax.fori_loop(0, peers, step, start)


def features(a):
    return jnp.where(a > 0, a + 1.0, jnp.exp(jnp.minimum(a, 0.0)))


def slope(a):
    return jnp.where(a > 0, 1.0, jnp.exp(jnp.minimum(a, 0.0)))


def add_pairs(earlier, later):
    return (earlier[0] + later[0], earlier[1] + later[1])


def per_device(frames, grad_frames, w_qkv, w_out):
    f32 = jnp.float32
    bf = jnp.bfloat16
    x = frames[0]
    dy = grad_frames[0]
    rows = x.shape[0]
    inner = HEADS * HEAD
    qkv = jnp.dot(x, w_qkv, preferred_element_type=f32).astype(bf)
    q = qkv[:, :inner].astype(f32)
    k = qkv[:, inner : 2 * inner].astype(f32)
    fq = features(q).astype(bf)
    fk = features(k).astype(bf)
    v = qkv[:, 2 * inner :]
    g = jnp.dot(dy, w_out, preferred_element_type=f32).astype(bf)
    nblk = rows // BLOCK
    shape4 = (nblk, BLOCK, HEADS, HEAD)
    fqb, fkb, vb, gb = (
        fq.reshape(shape4),
        fk.reshape(shape4),
        v.reshape(shape4),
        g.reshape(shape4),
    )
    mask = jnp.tril(jnp.ones((BLOCK, BLOCK), bool))
    state_add = jnp.einsum("nshd,nshe->nhde", fkb, vb, preferred_element_type=f32)
    norm_add = jnp.sum(fkb.astype(f32), 1)
    zeros_state = jnp.zeros((HEADS, HEAD, HEAD), f32)
    zeros_norm = jnp.zeros((HEADS, HEAD), f32)
    state_pre, norm_pre = prefix(
        (jnp.sum(state_add, 0), jnp.sum(norm_add, 0)),
        "tm",
        add_pairs,
        (zeros_state, zeros_norm),
        False,
    )

    def forward(carry, item_list):
        running_state, running_norm = carry
        (
            query_feature_map,
            value_rows,
            output_gradient_rows,
            state_increment,
            norm_increment,
            key_feature_map,
        ) = item_list
        fq32 = query_feature_map.astype(f32)
        g32 = output_gradient_rows.astype(f32)
        block_state = running_state.astype(bf)
        scores = jnp.where(
            mask,
            jnp.einsum(
                "thd,shd->hts", query_feature_map, key_feature_map, preferred_element_type=f32
            ),
            0.0,
        )
        den = scores.sum(-1).T + jnp.sum(fq32 * running_norm[None], -1)
        weights = scores.astype(bf)
        num = jnp.einsum(
            "hts,she->the", weights, value_rows, preferred_element_type=f32
        ) + jnp.einsum("thd,hde->the", query_feature_map, block_state, preferred_element_type=f32)
        ratio = num / den[..., None]
        attention_block = ratio.astype(bf)
        numerator_gradient = (g32 / den[..., None]).astype(bf)
        denominator_gradient = -jnp.sum(g32 * ratio, -1) / den
        block_score_gradient = jnp.einsum(
            "thd,the->hde", query_feature_map, numerator_gradient, preferred_element_type=f32
        )
        block_normalizer_gradient = jnp.sum(denominator_gradient[..., None] * fq32, 0)
        return (
            (running_state + state_increment, running_norm + norm_increment),
            (
                attention_block,
                block_state,
                running_norm,
                numerator_gradient,
                denominator_gradient,
                block_score_gradient,
                block_normalizer_gradient,
            ),
        )

    _, outs = lax.scan(forward, (state_pre, norm_pre), (fqb, vb, gb, state_add, norm_add, fkb))
    (
        attention_block,
        block_state,
        running_norm,
        numerator_gradient,
        denominator_gradient,
        block_score_gradient,
        block_normalizer_gradient,
    ) = outs
    dstate_suf, dnorm_suf = prefix(
        (jnp.sum(block_score_gradient, 0), jnp.sum(block_normalizer_gradient, 0)),
        "tm",
        add_pairs,
        (zeros_state, zeros_norm),
        True,
    )

    def backward(carry, item_list):
        dstate, dnorm = carry
        query_feature_map, key_feature_map, value_rows, sb, nz, dn, dd, dsb, dzb = item_list
        dstate_b = dstate.astype(bf)
        scores = jnp.where(
            mask,
            jnp.einsum(
                "thd,shd->hts", query_feature_map, key_feature_map, preferred_element_type=f32
            ),
            0.0,
        )
        weights = scores.astype(bf)
        dscore = (
            jnp.einsum("the,she->hts", dn, value_rows, preferred_element_type=f32)
            + dd.T[:, :, None]
        )
        dscore = jnp.where(mask, dscore, 0.0).astype(bf)
        dfq = (
            jnp.einsum("hts,shd->thd", dscore, key_feature_map, preferred_element_type=f32)
            + jnp.einsum("the,hde->thd", dn, sb, preferred_element_type=f32)
            + dd[..., None] * nz[None]
        )
        dfk = (
            jnp.einsum("hts,thd->shd", dscore, query_feature_map, preferred_element_type=f32)
            + jnp.einsum("she,hde->shd", value_rows, dstate_b, preferred_element_type=f32)
            + dnorm[None]
        )
        dv = jnp.einsum("hts,the->she", weights, dn, preferred_element_type=f32) + jnp.einsum(
            "shd,hde->she", key_feature_map, dstate_b, preferred_element_type=f32
        )
        return ((dstate + dsb, dnorm + dzb), (dfq, dfk, dv))

    _, grads = lax.scan(
        backward,
        (dstate_suf, dnorm_suf),
        (
            fqb,
            fkb,
            vb,
            block_state,
            running_norm,
            numerator_gradient,
            denominator_gradient,
            block_score_gradient,
            block_normalizer_gradient,
        ),
        reverse=True,
    )
    dfq, dfk, dv = grads
    dq = dfq.reshape(rows, inner) * slope(q)
    dk = dfk.reshape(rows, inner) * slope(k)
    dqkv = jnp.concatenate([dq, dk, dv.reshape(rows, inner)], axis=1).astype(bf)
    dx = lax.dot_general(dqkv, w_qkv, (((1,), (1,)), ((), ())), preferred_element_type=f32).astype(
        bf
    )
    attn_rows = attention_block.reshape(rows, inner)
    part_qkv = lax.dot_general(x, dqkv, (((0,), (0,)), ((), ())), preferred_element_type=f32)
    part_out = lax.dot_general(dy, attn_rows, (((0,), (0,)), ((), ())), preferred_element_type=f32)
    summed = lax.psum_scatter(
        jnp.concatenate([part_qkv, part_out], axis=1), ("tm", "dp"), scatter_dimension=0, tiled=True
    )
    summed = lax.all_gather(summed, "dp", axis=0, tiled=True)
    return (dx[None], summed[:, : 3 * inner], summed[:, 3 * inner :])


def solution(mesh):
    placed = (P("dp", "tm", None), P("dp", "tm", None), P(), P())
    return jax.shard_map(
        per_device,
        mesh=mesh,
        in_specs=placed,
        out_specs=(P("dp", "tm", None), P("tm", None), P("tm", None)),
        check_vma=False,
    )
```

profile of v0, /device:TPU:1, one launch (start us, length us, event | category | flops | bytes accessed | tf_op | source)
XLA Modules:
  0.0 380.2 jit_solution(3086311583857711741)
XLA Ops:
  7.2 3.3 convolution_convert_fusion
  11.8 1.0 fusion.40
  12.9 1.3 fusion.8
  15.2 1.1 copy.54
  16.3 27.5 %all_gather.20 = f32[8,12,64]{2,1,0:T(8,128)} all-gather(f32[1,12,64]{2,1,0:T(8,128)S(1)} %reduce_sum.66), channel_id=1, replica_groups=mesh['tm'=8,'dp'=4] {'tm'}, dimensions={0}, use_global_device_ids=true | all-gather | bytes 27648 | tf_op jit(solution)/shard_map/all_gather | solution.py:13
  44.9 1.0 fusion.28
  45.9 27.5 %all-gather.8.cloned.1.call-done = f32[96,64,64]{2,1,0:T(8,128)} async-done(((f32[12,64,64]{2,1,0:T(8,128)}), f32[96,64,64]{2,1,0:T(8,128)}) %all-gather.8.cloned.1.call-update) | async-done | bytes 1572880 | tf_op jit(solution)/shard_map/all_gather | solution.py:13
  73.5 14.9 %while.22 = (s32[]{:T(128)}, f32[12,64,64]{2,1,0:T(8,128)S(1)}, f32[12,64]{1,0:T(8,128)S(1)}, s32[]{:T(128)}, f32[8,12,64,64]{3,2,1,0:T(8,128)}, /*index=5*/f32[8,12,64]{2,1,0:T(8,128)}, s32[]{:T(128)}, s32[]{:T(128)}) while((s32[]{:T(128)}, f32[12,64,64]{2,1,0:T(8,128)S(1)}, f32[12,64]{1,0:T(8,128)S(1)}, s32[]{:T(128)}, ...), condition=%wide.region_3.4_spmd.clone, body=%wide.region_2.3_spmd.clone.sunk | while | flops 149764 | bytes 599163 | solution.py:26
  74.2 1.1 add_select_fusion.8
  76.1 1.1 add_select_fusion.8
  77.9 1.1 add_select_fusion.8
  79.8 1.1 add_select_fusion.8
  81.7 1.1 add_select_fusion.8
  83.5 1.1 add_select_fusion.8
  85.4 1.1 add_select_fusion.8
  87.3 1.1 add_select_fusion.8
  89.2 2.6 fusion.38
  92.4 1.0 fusion.43
  95.0 1.3 fusion.1
  96.5 1.9 fusion.5
  98.3 1.9 copy.60
  101.0 0.9 copy.62
  101.9 2.0 fusion.21
  104.0 27.1 %all_gather.22 = f32[8,12,64]{2,1,0:T(8,128)} all-gather(f32[1,12,64]{2,1,0:T(8,128)S(1)} %broadcast_in_dim.84), channel_id=1, replica_groups=mesh['tm'=8,'dp'=4] {'tm'}, dimensions={0}, use_global_device_ids=true | all-gather | bytes 27648 | tf_op jit(solution)/shard_map/all_gather | solution.py:13
  131.1 1.5 fusion.26
  132.5 2.1 fusion.42
  134.7 3.3 convolution_bitcast_fusion.1
  138.0 14.9 %all-gather.10.cloned.1.call-done = f32[96,64,64]{2,1,0:T(8,128)} async-done(((f32[12,64,64]{2,1,0:T(8,128)}), f32[96,64,64]{2,1,0:T(8,128)}) %all-gather.10.cloned.1.call-update) | async-done | bytes 1572880 | tf_op jit(solution)/shard_map/all_gather | solution.py:13
  152.8 14.9 %while.23 = (s32[]{:T(128)}, f32[12,64,64]{2,1,0:T(8,128)S(1)}, f32[12,64]{1,0:T(8,128)S(1)}, s32[]{:T(128)}, f32[8,12,64,64]{3,2,1,0:T(8,128)}, /*index=5*/f32[...) while((s32[]{:T(128)}, f32[12,64,64]{2,1,0:T(8,128)S(1)}, ...), condition=%wide.region_8.9_spmd.clone, body=%wide.region_7.8_spmd.clone.sunk | while | flops 149768 | bytes 599225 | solution.py:26
  153.5 1.1 add_select_fusion.10
  155.4 1.1 add_select_fusion.10
  157.3 1.1 add_select_fusion.10
  159.2 1.1 add_select_fusion.10
  161.0 1.1 add_select_fusion.10
  162.9 1.1 add_select_fusion.10
  164.8 1.1 add_select_fusion.10
  166.6 1.1 add_select_fusion.10
  167.8 0.9 fusion.7
  168.7 1.2 fusion.6
  170.2 1.1 copy.66
  171.3 2.6 convolution_bitcast_fusion
  173.9 7.0 %pad_maximum_fusion = f32[1024,3072]{0,1:T(8,128)} fusion(f32[1024,768]{0,1:T(8,128)S(1)} %copy-done.1, f32[1024,2304]{0,1:T(8,128)S(1)} %convolution_bitcast_fusion), kind=kLoop, calls=%fused_computation.4 | loop fusion | flops 3145728 | bytes 25165824 | tf_op jit(solution)/shard_map/concatenate | solution.py:199
  180.9 12.6 %copy.75 = f32[1024,3072]{1,0:T(8,128)} copy(f32[1024,3072]{0,1:T(8,128)} %pad_maximum_fusion) | data formatting | bytes 25165824
  193.6 153.5 %reduce-scatter.4.cloned.1.call-done = f32[32,3072]{1,0:T(8,128)} async-done(((f32[1024,3072]{1,0:T(8,128)}), f32[32,3072]{1,0:T(8,128)}) %reduce-scatter.4.cloned.1.call-update) | async-done | bytes 393232 | tf_op jit(solution)/shard_map/reduce_scatter | solution.py:198
  347.2 4.7 %fusion.9 = bf16[1,128,1024]{2,1,0:T(8,128)(2,1)} fusion(bf16[1024,2304]{1,0:T(8,128)(2,1)} %param.10, bf16[128,768]{1,0:T(8,128)(2,1)S(1)} %copy.66, bf16[128,768]{1,0:T(8,128)(2,1)S(1)} %fusion.15, bf16[128,768]{1,0:T(8,128)(2,1)S(1)} %copy-done.5), kind=kOutput, calls=%fused_computation.25 | convolution fusion | flops 605880320 | bytes 5570560 | tf_op jit(solution)/shard_map/dot_general | solution.py:192
  351.8 17.7 %all-gather.6.cloned.1.call-done = f32[128,3072]{1,0:T(8,128)} async-done(((f32[32,3072]{1,0:T(8,128)}), f32[128,3072]{1,0:T(8,128)}) %all-gather.6.cloned.1.call-update) | async-done | bytes 1572880 | tf_op jit(solution)/shard_map/all_gather | solution.py:201
  369.5 1.8 slice.24
  371.3 2.4 slice.23
  (69 shorter events, 19.0 us)
Async XLA Ops:
  7.2 5.7 %copy-start = (bf16[1024,768]{1,0:T(8,128)(2,1)S(1)}, bf16[1024,768]{1,0:T(8,128)(2,1)}, u32[]{:S(2)}) copy-start(bf16[1024,768]{1,0:T(8,128)(2,1)} %param.11) | copy-start | bytes 4718596
  7.2 66.3 %all-gather.8.cloned.1.call-start = ((), (), s32[]{:S(2)}) async-start(), calls=%async_computation.2 | async-start | bytes 3538944 | tf_op jit(solution)/shard_map/all_gather | solution.py:13
  12.8 140.0 %all-gather.10.cloned.1.call-start = ((), (), s32[]{:S(2)}) async-start(), calls=%async_computation.3 | async-start | bytes 3538944 | tf_op jit(solution)/shard_map/all_gather | solution.py:13
  43.8 29.6 %copy-start.11 = (pred[128,128]{0,1:T(8,128)(4,1)}, pred[128,128]{0,1:T(8,128)(4,1)S(1)}, u32[]{:S(2)}) copy-start(pred[128,128]{0,1:T(8,128)(4,1)S(1)} %iota_compare_fusion) | copy-start | bytes 49156
  44.2 0.7 copy-start.3
  44.2 44.4 %copy-start.10 = (f32[12,128]{1,0:T(8,128)}, f32[12,128]{1,0:T(8,128)S(1)}, u32[]{:S(2)}) copy-start(f32[12,128]{1,0:T(8,128)S(1)} %get-tuple-element.451) | copy-start | bytes 18436
  73.5 15.7 %copy-start.6 = (f32[128,768]{0,1:T(8,128)S(1)}, f32[128,768]{0,1:T(8,128)}, u32[]{:S(2)}) copy-start(f32[128,768]{0,1:T(8,128)} %copy.53) | copy-start | bytes 1179652
  88.6 0.6 copy-start.8
  88.6 3.1 copy-start.9
  91.7 0.7 copy-start.2
  93.4 253.7 %reduce-scatter.4.cloned.1.call-start = ((), (), s32[]{:S(2)}) async-start(), calls=%async_computation.4 | async-start | bytes 12976128 | tf_op jit(solution)/shard_map/reduce_scatter | solution.py:198
  94.2 4.1 %copy-start.7 = (f32[128,12]{0,1:T(8,128)}, f32[128,12]{0,1:T(8,128)S(1)}, u32[]{:S(2)}) copy-start(f32[128,12]{0,1:T(8,128)S(1)} %negate_divide_fusion) | copy-start | bytes 18436
  96.2 2.1 copy-start.4
  171.3 2.6 copy-start.1
  193.5 153.6 %copy-start.5 = (bf16[128,768]{1,0:T(8,128)(2,1)S(1)}, bf16[128,768]{1,0:T(8,128)(2,1)}, u32[]{:S(2)}) copy-start(bf16[128,768]{1,0:T(8,128)(2,1)} %get-tuple-element.445) | copy-start | bytes 589828
  193.5 176.0 %all-gather.6.cloned.1.call-start = ((), (), s32[]{:S(2)}) async-start(), calls=%async_computation.1 | async-start | bytes 1966080 | tf_op jit(solution)/shard_map/all_gather | solution.py:201
Sparse Core Ops, SparseCore 0:
  12.9 60.4 all-gather.7
  93.5 59.2 all-gather.9
  193.7 153.4 reduce-scatter.3
  348.5 20.9 all-gather.5
where the time goes:
time: 383 us; the launch traced here: 380 us
  waiting for transfers between devices  214 us (56%)
  blocking collectives  54.6 us (14%)
  other arithmetic  41.1 us (11%)
  matrix products  30.1 us (8%)
  local copies, waits for them, and re-layouts  26 us (7%)
  between operations  14 us (4%)
    reduce_scatter x1, waiting for transfers between devices, per_device(): lax.psum_scatter(jnp.concatenate([part_qkv, part_out], axis=1), ('tm', 'd...  154 us
    all_gather x2, blocking collectives, prefix(): everything = jax.tree.map(lambda part: lax.all_gather(part, axis), value)  54.6 us
    all_gather x2, waiting for transfers between devices, prefix(): everything = jax.tree.map(lambda part: lax.all_gather(part, axis), value)  42.4 us
    select_n x32, other arithmetic, step(): return jax.tree.map(lambda a, b: jnp.where(reached, a, b), new, before)  29.4 us
    all_gather x1, waiting for transfers between devices, per_device(): summed = lax.all_gather(summed, 'dp', axis=0, tiled=True)  17.7 us
    unnamed x25, local copies, waits for them, and re-layouts  14.6 us
  transfers between devices with their start and end apart: 4, of which 4 were waited for; matrix products, arithmetic and copies ran while one was open for 7% of the time, Pallas kernels for 0%

commit v1 on v0

v1 whole, which is shorter than its diff:
```python
import functools

import jax
import jax.numpy as jnp
from jax import lax
from jax.experimental import pallas as pl
from jax.experimental.pallas import tpu as pltpu
from jax.sharding import PartitionSpec as P

HEADS = 12
HEAD = 64
PAIR = 128
MESH = pl.DeviceIdType.MESH
f32 = jnp.float32
bf = jnp.bfloat16


def dot(a, b, ca=1, cb=0):
    return lax.dot_general(a, b, (((ca,), (cb,)), ((), ())), preferred_element_type=f32)


def kernel(
    tm, dp, chunks,
    x_hbm, dy_hbm, wq_hbm, wo_hbm,
    dx_ref, fin_ref,
    x_ref, dy_ref, wq_ref, wo_ref,
    xf, rx, fxt,
    fq, fk, v, g, slopes,
    w_sc, a_sc, den, num, dnum, dvi, dki, ddn,
    nrm, nrm_in, st, st_in, states,
    comb, fd_in, fdb,
    gbuf, rs_in, acc,
    lsem, nsend, nrecv, ssend, srecv, xsend, xrecv, fsend, frecv, rsend, rrecv, gsend, grecv,
):
    inner = HEADS * HEAD
    pairs = inner // PAIR
    bits = tm.bit_length() - 1
    i = lax.axis_index("tm")
    d = lax.axis_index("dp")
    rows = x_ref.shape[0]
    width = x_ref.shape[1]
    block = width // tm
    cols = 4 * inner // dp
    cc = cols // chunks

    loads = [
        pltpu.make_async_copy(src, dst, lsem.at[n])
        for n, (src, dst) in enumerate(
            ((x_hbm, x_ref), (dy_hbm, dy_ref), (wq_hbm, wq_ref), (wo_hbm, wo_ref))
        )
    ]
    for copy in loads:
        copy.start()

    barrier = pltpu.get_barrier_semaphore()
    for k in range(1, tm):
        pl.semaphore_signal(
            barrier, inc=1, device_id=(lax.rem(i + k, tm), d), device_id_type=MESH
        )
    for k in range(1, dp):
        pl.semaphore_signal(
            barrier, inc=1, device_id=(i, lax.rem(d + k, dp)), device_id_type=MESH
        )

    def to_dp(k, src, dst, send, recv):
        return pltpu.make_async_remote_copy(
            src_ref=src, dst_ref=dst, send_sem=send, recv_sem=recv,
            device_id=(i, lax.rem(d + k, dp)), device_id_type=MESH,
        )

    def to_tm(peer, src, dst, send, recv):
        return pltpu.make_async_remote_copy(
            src_ref=src, dst_ref=dst, send_sem=send, recv_sem=recv,
            device_id=(peer, d), device_id_type=MESH,
        )

    sent = []

    loads[0].wait()
    loads[1].wait()
    xf[0] = x_ref[...].astype(f32)
    xf[1] = dy_ref[...].astype(f32)
    pl.semaphore_wait(barrier, tm - 1 + dp - 1)

    def second(who):
        return (who * cols) // (3 * inner)

    early = []
    for k in range(1, dp):
        peer = lax.rem(d + k, dp)
        copy = to_dp(k, xf.at[second(peer)], rx.at[k - 1], xsend.at[k - 1], xrecv.at[k - 1])
        copy.start()
        early.append(copy)
    sent += early

    lane = lax.broadcasted_iota(jnp.int32, (rows, PAIR), 1)
    lo = lane < HEAD
    lo_half = lo[:HEAD]
    tri = lax.broadcasted_iota(jnp.int32, (rows, rows), 0) >= lax.broadcasted_iota(
        jnp.int32, (rows, rows), 1
    )

    def at(p):
        return pl.ds(p * PAIR, PAIR)

    def pack(s):
        return jnp.where(lo_half, s[:HEAD], s[HEAD:])

    def unpack(s):
        zero = jnp.zeros_like(s)
        return jnp.concatenate(
            [jnp.where(lo_half, s, zero), jnp.where(lo_half, zero, s)], axis=0
        ).astype(bf)

    def keep_lo(a):
        return jnp.where(lo, a, jnp.zeros_like(a))

    def keep_hi(a):
        return jnp.where(lo, jnp.zeros_like(a), a)

    def per_head_sum(a):
        first = jnp.sum(jnp.where(lo, a, 0.0), axis=1, keepdims=True)
        both = jnp.sum(jnp.where(lo, 0.0, a), axis=1, keepdims=True)
        return jnp.where(lo, first, both)

    def features(a):
        return jnp.where(a > 0, a + 1.0, jnp.exp(jnp.minimum(a, 0.0)))

    loads[2].wait()
    x = x_ref[...]
    kk = features(dot(x, wq_ref[:, inner : 2 * inner]).astype(bf).astype(f32))
    slopes[1] = jnp.minimum(kk, 1.0)
    fk[...] = kk.astype(bf)
    v[...] = dot(x, wq_ref[:, 2 * inner :]).astype(bf)
    nrm[0] = jnp.sum(fk[...].astype(f32), axis=0, keepdims=True)

    def direct(which):
        out = []
        for k in range(1, tm):
            copy = to_tm(
                lax.rem(i + k, tm), nrm.at[which], nrm_in.at[which, k - 1],
                nsend.at[which, k - 1], nrecv.at[which, k - 1],
            )
            copy.start()
            out.append(copy)
        return out

    norm_copies = direct(0)
    sent += norm_copies

    def direct_sum(which, copies, earlier):
        total = jnp.zeros((1, inner), f32)
        for k, copy in enumerate(copies):
            copy.wait_recv()
            reached = (i - (k + 1) >= 0) if earlier else (i - (k + 1) < 0)
            total = total + jnp.where(reached, nrm_in[which, k], 0.0)
        return total

    for p in range(pairs):
        st[0, 0, pl.ds(p * HEAD, HEAD), :] = pack(dot(fk[:, at(p)], v[:, at(p)], 0, 0))

    def hop(which, b):
        peer = i + (1 << b) - 2 * (i & (1 << b))
        copy = to_tm(
            peer, st.at[which, b], st_in.at[which, b], ssend.at[which, b], srecv.at[which, b]
        )
        copy.start()
        return copy

    def last_hop():
        b = bits - 1
        bit = (i >> b) & 1
        peer = i + (1 << b) - 2 * (i & (1 << b))
        copy = to_tm(
            peer, st.at[bit, b], st_in.at[0, b], ssend.at[0, b], srecv.at[0, b]
        )
        copy.start()
        return copy

    def arrive(which, b, copy):
        copy.wait_recv()
        bit = (i >> b) & 1
        use = (bit == 1) if which == 0 else (bit == 0)
        got = st_in[which, b]
        add = jnp.where(use, got, 0.0)
        states[which] = add if b == 0 else states[which] + add
        st[which, b + 1] = st[which, b] + got

    hops = [None, None]
    hops[0] = hop(0, 0)
    sent.append(hops[0])

    qq = features(dot(x, wq_ref[:, :inner]).astype(bf).astype(f32))
    slopes[0] = jnp.minimum(qq, 1.0)
    fq[...] = qq.astype(bf)
    loads[3].wait()
    g[...] = dot(dy_ref[...], wo_ref[...]).astype(bf)

    for p in range(pairs):
        q_p, k_p, v_p = fq[:, at(p)], fk[:, at(p)], v[:, at(p)]
        s0 = jnp.where(tri, dot(keep_lo(q_p), k_p, 1, 1), 0.0)
        s1 = jnp.where(tri, dot(keep_hi(q_p), k_p, 1, 1), 0.0)
        den[:, at(p)] = jnp.where(
            lo, jnp.sum(s0, axis=1, keepdims=True), jnp.sum(s1, axis=1, keepdims=True)
        )
        w0, w1 = s0.astype(bf), s1.astype(bf)
        w_sc[2 * p] = w0
        w_sc[2 * p + 1] = w1
        num[:, at(p)] = jnp.where(lo, dot(w0, v_p), dot(w1, v_p))

    norm_in = direct_sum(0, norm_copies, True)

    for p in range(pairs):
        q_p, v_p = fq[:, at(p)], v[:, at(p)]
        total = den[:, at(p)] + per_head_sum(
            q_p.astype(f32) * norm_in[:, p * PAIR : (p + 1) * PAIR]
        )
        inverse = 1.0 / total
        den[:, at(p)] = inverse
        dn = (g[:, at(p)].astype(f32) * inverse).astype(bf)
        dnum[:, at(p)] = dn
        st[1, 0, pl.ds(p * HEAD, HEAD), :] = pack(dot(q_p, dn, 0, 0))
    hops[1] = hop(1, 0)
    sent.append(hops[1])

    for p in range(pairs):
        v_p, dn = v[:, at(p)], dnum[:, at(p)]
        a_sc[2 * p] = dot(keep_lo(dn), v_p, 1, 1)
        a_sc[2 * p + 1] = dot(keep_hi(dn), v_p, 1, 1)
        dvi[:, at(p)] = jnp.where(
            lo, dot(w_sc[2 * p], dn, 0, 0), dot(w_sc[2 * p + 1], dn, 0, 0)
        )

    for b in range(bits - 1):
        for which in (0, 1):
            arrive(which, b, hops[which])
            if b < bits - 2:
                hops[which] = hop(which, b + 1)
                sent.append(hops[which])
    last = last_hop()
    sent.append(last)

    def reverse(n):
        out = 0
        for b in range(bits):
            out = out * 2 + ((n >> b) & 1)
        return out

    def place(k, value):
        turned = value.T.astype(bf)
        for n in range(tm):
            r = reverse(n)
            fxt[n * block : (n + 1) * block, k * rows : (k + 1) * rows] = turned[
                r * block : (r + 1) * block
            ]

    place(0, xf[second(d)])
    for k in range(1, dp):
        early[k - 1].wait_recv()
        place(k, rx[k - 1])

    last.wait_recv()
    bit = (i >> (bits - 1)) & 1
    got = st_in[0, bits - 1]
    before = jnp.where(bit == 1, got, 0.0)
    after = jnp.where(bit == 0, got, 0.0)
    if bits > 1:
        before = states[0] + before
        after = states[1] + after
    states[0] = before
    states[1] = after

    for p in range(pairs):
        s_b = unpack(states[0, pl.ds(p * HEAD, HEAD), :])
        q_p = fq[:, at(p)]
        inverse = den[:, at(p)]
        ratio = (num[:, at(p)] + dot(q_p, s_b)) * inverse
        comb[:, pl.ds(3 * inner + p * PAIR, PAIR)] = ratio.astype(bf).astype(f32)
        dd = -per_head_sum(g[:, at(p)].astype(f32) * ratio) * inverse
        ddn[:, at(p)] = dd
        nrm[1, :, at(p)] = jnp.sum(dd * q_p.astype(f32), axis=0, keepdims=True)
    dnorm_copies = direct(1)
    sent += dnorm_copies

    for p in range(pairs):
        s_b = unpack(states[0, pl.ds(p * HEAD, HEAD), :])
        ds_b = unpack(states[1, pl.ds(p * HEAD, HEAD), :])
        q_p, k_p, v_p, dn, dd = fq[:, at(p)], fk[:, at(p)], v[:, at(p)], dnum[:, at(p)], ddn[:, at(p)]
        d0 = jnp.where(tri, a_sc[2 * p] + dd[:, :1], 0.0).astype(bf)
        d1 = jnp.where(tri, a_sc[2 * p + 1] + dd[:, HEAD : HEAD + 1], 0.0).astype(bf)
        dq = (
            jnp.where(lo, dot(d0, k_p), dot(d1, k_p))
            + dot(dn, s_b, 1, 1)
            + dd * norm_in[:, p * PAIR : (p + 1) * PAIR]
        )
        comb[:, at(p)] = (dq * slopes[0, :, at(p)]).astype(bf).astype(f32)
        dki[:, at(p)] = jnp.where(lo, dot(d0, q_p, 0, 0), dot(d1, q_p, 0, 0)) + dot(
            v_p, ds_b, 1, 1
        )
        dv = dvi[:, at(p)] + dot(k_p, ds_b)
        comb[:, pl.ds(2 * inner + p * PAIR, PAIR)] = dv.astype(bf).astype(f32)
    dnorm = direct_sum(1, dnorm_copies, False)
    comb[:, pl.ds(inner, inner)] = ((dki[...] + dnorm) * slopes[1]).astype(bf).astype(f32)

    factors = []
    for j in range(chunks):
        row = []
        for k in range(1, dp):
            peer = lax.rem(d + k, dp)
            start = pl.multiple_of(peer * cols + j * cc, PAIR)
            copy = to_dp(
                k, comb.at[:, pl.ds(start, cc)], fd_in.at[j, k - 1],
                fsend.at[j, k - 1], frecv.at[j, k - 1],
            )
            copy.start()
            row.append(copy)
        factors.append(row)
        sent += row

    dx_ref[...] = dot(comb[:, : 3 * inner].astype(bf), wq_ref[...], 1, 1).astype(bf)

    def halving(j, s):
        half = width >> (s + 1)
        bit = (i >> s) & 1
        peer = i + (1 << s) - 2 * (i & (1 << s))
        other = pl.multiple_of((1 - bit) * half, block)
        source = gbuf.at[j] if s == 0 else acc[s - 1].at[j]
        copy = to_tm(
            peer, source.at[pl.ds(other, half), :], rs_in[s].at[j],
            rsend.at[j, s], rrecv.at[j, s],
        )
        copy.start()
        sent.append(copy)
        return copy

    moving = {}
    for j in range(chunks):
        mine = pl.multiple_of(d * cols + j * cc, PAIR)
        fdb[0:rows, :] = comb[:, pl.ds(mine, cc)].astype(bf)
        for k in range(1, dp):
            factors[j][k - 1].wait_recv()
            fdb[k * rows : (k + 1) * rows, :] = fd_in[j, k - 1].astype(bf)
        gbuf[j] = dot(fxt[...], fdb[...])
        moving[j, 0] = halving(j, 0)

    gathers = []
    order = sorted(
        ((j, s) for j in range(chunks) for s in range(bits)), key=lambda e: 10 * e[0] + 6 * e[1]
    )
    for j, s in order:
        moving[j, s].wait_recv()
        half = width >> (s + 1)
        mine = pl.multiple_of(((i >> s) & 1) * half, block)
        source = gbuf.at[j] if s == 0 else acc[s - 1].at[j]
        acc[s][j] = source[pl.ds(mine, half), :] + rs_in[s][j]
        if s + 1 < bits:
            moving[j, s + 1] = halving(j, s + 1)
        else:
            start = pl.multiple_of(d * cols + j * cc, PAIR)
            spot = fin_ref.at[:, pl.ds(start, cc)]
            for k in range(1, dp):
                copy = to_dp(k, acc[s].at[j], spot, gsend.at[j, k - 1], grecv.at[j, k - 1])
                copy.start()
                gathers.append(copy)
            spot[...] = acc[s][j]
    sent += gathers
    for copy in gathers:
        copy.wait_recv()
    for copy in sent:
        copy.wait_send()


def per_device(tm, dp, frames, grad_frames, w_qkv, w_out):
    x, dy = frames[0], grad_frames[0]
    rows, width = x.shape
    inner = HEADS * HEAD
    cols = 4 * inner // dp
    chunks = 3
    cc = cols // chunks
    bits = tm.bit_length() - 1
    block = width // tm
    pairs = inner // PAIR
    dma = pltpu.SemaphoreType.DMA

    def vm(shape, kind=f32):
        return pltpu.VMEM(shape, kind)

    dx, fin = pl.pallas_call(
        functools.partial(kernel, tm, dp, chunks),
        out_shape=(
            jax.ShapeDtypeStruct((rows, width), bf),
            jax.ShapeDtypeStruct((block, 4 * inner), f32),
        ),
        in_specs=[pl.BlockSpec(memory_space=pl.ANY)] * 4,
        out_specs=[pl.BlockSpec(memory_space=pltpu.VMEM)] * 2,
        scratch_shapes=[
            vm((rows, width), bf), vm((rows, width), bf),
            vm(w_qkv.shape, bf), vm(w_out.shape, bf),
            vm((2, rows, width)), vm((dp - 1, rows, width)), vm((width, dp * rows), bf),
            vm((rows, inner), bf), vm((rows, inner), bf), vm((rows, inner), bf),
            vm((rows, inner), bf), vm((2, rows, inner)),
            vm((HEADS, rows, rows), bf), vm((HEADS, rows, rows)),
            vm((rows, inner)), vm((rows, inner)), vm((rows, inner), bf),
            vm((rows, inner)), vm((rows, inner)), vm((rows, inner)),
            vm((2, 1, inner)), vm((2, tm - 1, 1, inner)),
            vm((2, bits, pairs * HEAD, PAIR)), vm((2, bits, pairs * HEAD, PAIR)),
            vm((2, pairs * HEAD, PAIR)),
            vm((rows, 4 * inner)), vm((chunks, dp - 1, rows, cc)), vm((dp * rows, cc), bf),
            vm((chunks, width, cc)),
            [vm((chunks, width >> (s + 1), cc)) for s in range(bits)],
            [vm((chunks, width >> (s + 1), cc)) for s in range(bits)],
            dma((4,)),
            dma((2, tm - 1)), dma((2, tm - 1)),
            dma((2, bits)), dma((2, bits)),
            dma((dp - 1,)), dma((dp - 1,)),
            dma((chunks, dp - 1)), dma((chunks, dp - 1)),
            dma((chunks, bits)), dma((chunks, bits)),
            dma((chunks, dp - 1)), dma((chunks, dp - 1)),
        ],
        compiler_params=pltpu.CompilerParams(
            collective_id=0, has_side_effects=True, vmem_limit_bytes=60 * 1024 * 1024
        ),
    )(x, dy, w_qkv, w_out)
    return (dx[None], fin[:, : 3 * inner], fin[:, 3 * inner :])


def solution(mesh):
    placed = (P("dp", "tm", None), P("dp", "tm", None), P(), P())
    return jax.shard_map(
        functools.partial(per_device, mesh.shape["tm"], mesh.shape["dp"]),
        mesh=mesh,
        in_specs=placed,
        out_specs=(P("dp", "tm", None), P("tm", None), P("tm", None)),
        check_vma=False,
    )
```

time: 383 us -> 107 us (0.28)
  waiting for transfers between devices: 214 us -> 0 us
  Pallas kernels: 0 us -> 101 us
  blocking collectives: 54.6 us -> 0 us
  other arithmetic: 41.1 us -> 0 us
  matrix products: 30.1 us -> 0 us
  local copies, waits for them, and re-layouts: 26 us -> 4.87 us
  between operations: 14 us -> 0.65 us
    reduce_scatter x1 -> x0, waiting for transfers between devices: 154 us -> none  [per_device(): lax.psum_scatter(jnp.concatenate([part_qkv, part_out], axis=1), ('tm', 'd...]
    pallas_call x0 -> x1, Pallas kernels: none -> 101 us  [per_device(): pl.pallas_call(functools.partial(kernel, tm, dp, chunks), out_shape=(jax....]
    all_gather x3 -> x0, waiting for transfers between devices: 60.1 us -> none  [the longest x2 42.4 us: prefix(): everything = jax.tree.map(lambda part: lax.all_gather(part, axis), value)]
    all_gather x2 -> x0, blocking collectives: 54.6 us -> none  [prefix(): everything = jax.tree.map(lambda part: lax.all_gather(part, axis), value)]
    dot_general x17 -> x0, matrix products: 30.1 us -> none  [the longest x1 4.68 us: per_device(): lax.dot_general(dqkv, w_qkv, (((1,), (1,)), ((), ())), preferred_element_...]
    select_n x32 -> x0, other arithmetic: 29.4 us -> none  [step(): return jax.tree.map(lambda a, b: jnp.where(reached, a, b), new, before)]
    unnamed x25 -> x3, local copies, waits for them, and re-layouts: 14.6 us -> 0.71 us
    concatenate x1 -> x0, other arithmetic: 7.03 us -> none  [per_device(): jnp.concatenate([part_qkv, part_out], axis=1)]
  transfers between devices with their start and end apart: 4 -> 0, of which waited for: 4 -> 0; matrix products, arithmetic and copies ran while one was open for 7% -> 0% of each run, Pallas kernels for 0% -> 0%
where the time goes in v1:
time: 107 us; the launch traced here: 106 us
  Pallas kernels  101 us (94%)
  local copies, waits for them, and re-layouts  4.87 us (5%)
    pallas_call x1, Pallas kernels, per_device(): pl.pallas_call(functools.partial(kernel, tm, dp, chunks), out_shape=(jax....  101 us
    slice x2, local copies, waits for them, and re-layouts, per_device(): return (dx[None], fin[:, :3 * inner], fin[:, 3 * inner:])  4.17 us

profile of v1, /device:TPU:1, one launch (start us, length us, event | category | flops | bytes accessed | tf_op | source)
XLA Modules:
  0.0 106.4 jit_solution(15871217871150401229)
XLA Ops:
  0.6 100.9 %shard_map.67 = (bf16[128,1024]{1,0:T(8,128)(2,1)}, f32[128,3072]{1,0:T(8,128)}) custom-call(bf16[128,1024]{1,0:T(8,128)(2,1)} %bitcast.4, bf16[128,1024]{1,0:T(8,128)(2,1)} %bitcast.5, bf16[1024,2304]{1,0:T(8,128)(2,1)} %wq_hbm.1, bf16[1024,768]{1,0:T(8,128)(2,1)} %wo_hbm.1), custom_call_target="tpu_custom_call" | custom-call | tf_op jit(solution)/shard_map/pallas_call | solution.py:388
  101.5 0.0 copy-start
  101.6 1.8 %slice.7 = f32[128,768]{1,0:T(8,128)} slice(f32[128,3072]{1,0:T(8,128)} %get-tuple-element.6), slice={[0:128], [2304:3072]} | slice | bytes 786432 | tf_op jit(solution)/shard_map/slice | solution.py:424
  103.4 2.4 %slice.6 = f32[128,2304]{1,0:T(8,128)} slice(f32[128,3072]{1,0:T(8,128)} %get-tuple-element.6), slice={[0:128], [0:2304]} | slice | bytes 2359296 | tf_op jit(solution)/shard_map/slice | solution.py:424
  105.7 0.0 copy-done
  105.7 0.7 copy.8
Async XLA Ops:
  101.5 4.2 %copy-start = (bf16[128,1024]{1,0:T(8,128)(2,1)S(1)}, bf16[128,1024]{1,0:T(8,128)(2,1)}, u32[]{:S(2)}) copy-start(bf16[128,1024]{1,0:T(8,128)(2,1)} %get-tuple-element.5) | copy-start | bytes 786436

commit v2 on v1

--- a/solution.py
+++ b/solution.py
@@ -46,7 +46,13 @@
     loads = [
         pltpu.make_async_copy(src, dst, lsem.at[n])
         for n, (src, dst) in enumerate(
-            ((x_hbm, x_ref), (dy_hbm, dy_ref), (wq_hbm, wq_ref), (wo_hbm, wo_ref))
+            (
+                (x_hbm, x_ref),
+                (dy_hbm, dy_ref),
+                (wq_hbm.at[:, pl.ds(inner, 2 * inner)], wq_ref.at[:, pl.ds(inner, 2 * inner)]),
+                (wq_hbm.at[:, pl.ds(0, inner)], wq_ref.at[:, pl.ds(0, inner)]),
+                (wo_hbm, wo_ref),
+            )
         )
     ]
     for copy in loads:
@@ -190,10 +196,11 @@
     hops[0] = hop(0, 0)
     sent.append(hops[0])
 
+    loads[3].wait()
     qq = features(dot(x, wq_ref[:, :inner]).astype(bf).astype(f32))
     slopes[0] = jnp.minimum(qq, 1.0)
     fq[...] = qq.astype(bf)
-    loads[3].wait()
+    loads[4].wait()
     g[...] = dot(dy_ref[...], wo_ref[...]).astype(bf)
 
     for p in range(pairs):
@@ -255,9 +262,6 @@
             ]
 
     place(0, xf[second(d)])
-    for k in range(1, dp):
-        early[k - 1].wait_recv()
-        place(k, rx[k - 1])
 
     last.wait_recv()
     bit = (i >> (bits - 1)) & 1
@@ -299,6 +303,9 @@
         )
         dv = dvi[:, at(p)] + dot(k_p, ds_b)
         comb[:, pl.ds(2 * inner + p * PAIR, PAIR)] = dv.astype(bf).astype(f32)
+    for k in range(1, dp):
+        early[k - 1].wait_recv()
+        place(k, rx[k - 1])
     dnorm = direct_sum(1, dnorm_copies, False)
     comb[:, pl.ds(inner, inner)] = ((dki[...] + dnorm) * slopes[1]).astype(bf).astype(f32)
 
@@ -317,12 +324,16 @@
         factors.append(row)
         sent += row
 
-    dx_ref[...] = dot(comb[:, : 3 * inner].astype(bf), wq_ref[...], 1, 1).astype(bf)
+    plain = tuple(range(bits))
+    orders = [plain] * chunks
+    if chunks >= 6:
+        orders[1] = plain[1:] + plain[:1]
 
     def halving(j, s):
         half = width >> (s + 1)
-        bit = (i >> s) & 1
-        peer = i + (1 << s) - 2 * (i & (1 << s))
+        b = orders[j][s]
+        bit = (i >> b) & 1
+        peer = i + (1 << b) - 2 * (i & (1 << b))
         other = pl.multiple_of((1 - bit) * half, block)
         source = gbuf.at[j] if s == 0 else acc[s - 1].at[j]
         copy = to_tm(
@@ -334,23 +345,30 @@
         return copy
 
     moving = {}
-    for j in range(chunks):
+    gathers = []
+
+    def multiply(j):
         mine = pl.multiple_of(d * cols + j * cc, PAIR)
         fdb[0:rows, :] = comb[:, pl.ds(mine, cc)].astype(bf)
         for k in range(1, dp):
             factors[j][k - 1].wait_recv()
             fdb[k * rows : (k + 1) * rows, :] = fd_in[j, k - 1].astype(bf)
-        gbuf[j] = dot(fxt[...], fdb[...])
+        product = dot(fxt[...], fdb[...])
+        if orders[j] == plain:
+            gbuf[j] = product
+        else:
+            for n in range(tm):
+                r = reverse(n)
+                to = 0
+                for b in orders[j]:
+                    to = to * 2 + ((r >> b) & 1)
+                gbuf[j, to * block : (to + 1) * block] = product[n * block : (n + 1) * block]
         moving[j, 0] = halving(j, 0)
 
-    gathers = []
-    order = sorted(
-        ((j, s) for j in range(chunks) for s in range(bits)), key=lambda e: 10 * e[0] + 6 * e[1]
-    )
-    for j, s in order:
+    def reduce(j, s):
         moving[j, s].wait_recv()
         half = width >> (s + 1)
-        mine = pl.multiple_of(((i >> s) & 1) * half, block)
+        mine = pl.multiple_of(((i >> orders[j][s]) & 1) * half, block)
         source = gbuf.at[j] if s == 0 else acc[s - 1].at[j]
         acc[s][j] = source[pl.ds(mine, half), :] + rs_in[s][j]
         if s + 1 < bits:
@@ -363,6 +381,24 @@
                 copy.start()
                 gathers.append(copy)
             spot[...] = acc[s][j]
+
+    def input_gradient():
+        dx_ref[...] = dot(comb[:, : 3 * inner].astype(bf), wq_ref[...], 1, 1).astype(bf)
+
+    events = [(4.0, input_gradient, ())]
+    rank = 0
+    for j in range(chunks):
+        events.append((2.8 * j, multiply, (j,)))
+        if orders[j] == plain:
+            rank += 1
+            for s in range(bits):
+                events.append((1.6 + 5.6 * rank + 4.5 * s, reduce, (j, s)))
+        else:
+            for s in range(bits):
+                late = 5.6 * chunks if s == bits - 1 else 10.0 + 6.0 * s
+                events.append((1.6 + late, reduce, (j, s)))
+    for _, act, what in sorted(events, key=lambda e: e[0]):
+        act(*what)
     sent += gathers
     for copy in gathers:
         copy.wait_recv()
@@ -375,7 +411,7 @@
     rows, width = x.shape
     inner = HEADS * HEAD
     cols = 4 * inner // dp
-    chunks = 3
+    chunks = cols // PAIR
     cc = cols // chunks
     bits = tm.bit_length() - 1
     block = width // tm
@@ -409,7 +445,7 @@
             vm((chunks, width, cc)),
             [vm((chunks, width >> (s + 1), cc)) for s in range(bits)],
             [vm((chunks, width >> (s + 1), cc)) for s in range(bits)],
-            dma((4,)),
+            dma((5,)),
             dma((2, tm - 1)), dma((2, tm - 1)),
             dma((2, bits)), dma((2, bits)),
             dma((dp - 1,)), dma((dp - 1,)),

time: 107 us -> 96.8 us (0.905)
  Pallas kernels: 101 us -> 91.1 us
    pallas_call x1, Pallas kernels: 101 us -> 91.1 us  [per_device(): pl.pallas_call(functools.partial(kernel, tm, dp, chunks), out_shape=(jax....]
where the time goes in v2:
time: 96.8 us; the launch traced here: 96.6 us
  Pallas kernels  91.1 us (94%)
  local copies, waits for them, and re-layouts  4.87 us (5%)
    pallas_call x1, Pallas kernels, per_device(): pl.pallas_call(functools.partial(kernel, tm, dp, chunks), out_shape=(jax....  91.1 us
    slice x2, local copies, waits for them, and re-layouts, per_device(): return (dx[None], fin[:, :3 * inner], fin[:, 3 * inner:])  4.17 us

profile of v2, /device:TPU:1, one launch (start us, length us, event | category | flops | bytes accessed | tf_op | source)
XLA Modules:
  0.0 96.6 jit_solution(14688344604017205840)
XLA Ops:
  0.6 91.1 %shard_map.67 = (bf16[128,1024]{1,0:T(8,128)(2,1)}, f32[128,3072]{1,0:T(8,128)}) custom-call(bf16[128,1024]{1,0:T(8,128)(2,1)} %bitcast.4, bf16[128,1024]{1,0:T(8,128)(2,1)} %bitcast.5, bf16[1024,2304]{1,0:T(8,128)(2,1)} %wq_hbm.1, bf16[1024,768]{1,0:T(8,128)(2,1)} %wo_hbm.1), custom_call_target="tpu_custom_call" | custom-call | tf_op jit(solution)/shard_map/pallas_call | solution.py:424
  91.7 0.0 copy-start
  91.7 1.8 %slice.7 = f32[128,768]{1,0:T(8,128)} slice(f32[128,3072]{1,0:T(8,128)} %get-tuple-element.6), slice={[0:128], [2304:3072]} | slice | bytes 786432 | tf_op jit(solution)/shard_map/slice | solution.py:460
  93.5 2.4 %slice.6 = f32[128,2304]{1,0:T(8,128)} slice(f32[128,3072]{1,0:T(8,128)} %get-tuple-element.6), slice={[0:128], [0:2304]} | slice | bytes 2359296 | tf_op jit(solution)/shard_map/slice | solution.py:460
  95.9 0.0 copy-done
  95.9 0.7 copy.8
Async XLA Ops:
  91.7 4.2 %copy-start = (bf16[128,1024]{1,0:T(8,128)(2,1)S(1)}, bf16[128,1024]{1,0:T(8,128)(2,1)}, u32[]{:S(2)}) copy-start(bf16[128,1024]{1,0:T(8,128)(2,1)} %get-tuple-element.5) | copy-start | bytes 786436

commit v3 on v2

--- a/solution.py
+++ b/solution.py
@@ -162,39 +162,39 @@
             total = total + jnp.where(reached, nrm_in[which, k], 0.0)
         return total
 
-    for p in range(pairs):
-        st[0, 0, pl.ds(p * HEAD, HEAD), :] = pack(dot(fk[:, at(p)], v[:, at(p)], 0, 0))
-
-    def hop(which, b):
+    def part(p):
+        return pl.ds(p * HEAD, HEAD)
+
+    def exchange(which, b, p, slot):
         peer = i + (1 << b) - 2 * (i & (1 << b))
         copy = to_tm(
-            peer, st.at[which, b], st_in.at[which, b], ssend.at[which, b], srecv.at[which, b]
+            peer, st.at[which, b, part(p)], st_in.at[slot, b, part(p)],
+            ssend.at[slot, b, p], srecv.at[slot, b, p],
         )
         copy.start()
-        return copy
-
-    def last_hop():
-        b = bits - 1
-        bit = (i >> b) & 1
-        peer = i + (1 << b) - 2 * (i & (1 << b))
-        copy = to_tm(
-            peer, st.at[bit, b], st_in.at[0, b], ssend.at[0, b], srecv.at[0, b]
-        )
-        copy.start()
-        return copy
-
-    def arrive(which, b, copy):
-        copy.wait_recv()
+        sent.append(copy)
+        hops[slot, b, p] = copy
+
+    def hop(which, b, p):
+        if b < bits - 1:
+            exchange(which, b, p, which)
+        elif which == 1:
+            exchange((i >> b) & 1, b, p, 0)
+
+    def arrive(which, b, p):
+        hops[which, b, p].wait_recv()
         bit = (i >> b) & 1
         use = (bit == 1) if which == 0 else (bit == 0)
-        got = st_in[which, b]
+        got = st_in[which, b, part(p)]
         add = jnp.where(use, got, 0.0)
-        states[which] = add if b == 0 else states[which] + add
-        st[which, b + 1] = st[which, b] + got
-
-    hops = [None, None]
-    hops[0] = hop(0, 0)
-    sent.append(hops[0])
+        states[which, part(p)] = add if b == 0 else states[which, part(p)] + add
+        st[which, b + 1, part(p)] = st[which, b, part(p)] + got
+        hop(which, b + 1, p)
+
+    hops = {}
+    for p in range(pairs):
+        st[0, 0, part(p)] = pack(dot(fk[:, at(p)], v[:, at(p)], 0, 0))
+        hop(0, 0, p)
 
     loads[3].wait()
     qq = features(dot(x, wq_ref[:, :inner]).astype(bf).astype(f32))
@@ -215,6 +215,9 @@
         w_sc[2 * p + 1] = w1
         num[:, at(p)] = jnp.where(lo, dot(w0, v_p), dot(w1, v_p))
 
+    if bits > 1:
+        for p in range(pairs):
+            arrive(0, 0, p)
     norm_in = direct_sum(0, norm_copies, True)
 
     for p in range(pairs):
@@ -226,9 +229,8 @@
         den[:, at(p)] = inverse
         dn = (g[:, at(p)].astype(f32) * inverse).astype(bf)
         dnum[:, at(p)] = dn
-        st[1, 0, pl.ds(p * HEAD, HEAD), :] = pack(dot(q_p, dn, 0, 0))
-    hops[1] = hop(1, 0)
-    sent.append(hops[1])
+        st[1, 0, part(p)] = pack(dot(q_p, dn, 0, 0))
+        hop(1, 0, p)
 
     for p in range(pairs):
         v_p, dn = v[:, at(p)], dnum[:, at(p)]
@@ -238,14 +240,14 @@
             lo, dot(w_sc[2 * p], dn, 0, 0), dot(w_sc[2 * p + 1], dn, 0, 0)
         )
 
-    for b in range(bits - 1):
-        for which in (0, 1):
-            arrive(which, b, hops[which])
-            if b < bits - 2:
-                hops[which] = hop(which, b + 1)
-                sent.append(hops[which])
-    last = last_hop()
-    sent.append(last)
+    waits = [
+        (4.0 * which + 0.7 * p + 2.4 * b, which, b, p)
+        for which in (0, 1)
+        for b in range(1 - which, bits - 1)
+        for p in range(pairs)
+    ]
+    for _, which, b, p in sorted(waits):
+        arrive(which, b, p)
 
     def reverse(n):
         out = 0
@@ -263,19 +265,22 @@
 
     place(0, xf[second(d)])
 
-    last.wait_recv()
-    bit = (i >> (bits - 1)) & 1
-    got = st_in[0, bits - 1]
-    before = jnp.where(bit == 1, got, 0.0)
-    after = jnp.where(bit == 0, got, 0.0)
-    if bits > 1:
-        before = states[0] + before
-        after = states[1] + after
-    states[0] = before
-    states[1] = after
-
-    for p in range(pairs):
-        s_b = unpack(states[0, pl.ds(p * HEAD, HEAD), :])
+    top = (i >> (bits - 1)) & 1
+
+    def settle(p):
+        hops[0, bits - 1, p].wait_recv()
+        got = st_in[0, bits - 1, part(p)]
+        before = jnp.where(top == 1, got, 0.0)
+        after = jnp.where(top == 0, got, 0.0)
+        if bits > 1:
+            before = states[0, part(p)] + before
+            after = states[1, part(p)] + after
+        states[0, part(p)] = before
+        states[1, part(p)] = after
+
+    for p in range(pairs):
+        settle(p)
+        s_b = unpack(states[0, part(p)])
         q_p = fq[:, at(p)]
         inverse = den[:, at(p)]
         ratio = (num[:, at(p)] + dot(q_p, s_b)) * inverse
@@ -447,7 +452,7 @@
             [vm((chunks, width >> (s + 1), cc)) for s in range(bits)],
             dma((5,)),
             dma((2, tm - 1)), dma((2, tm - 1)),
-            dma((2, bits)), dma((2, bits)),
+            dma((2, bits, pairs)), dma((2, bits, pairs)),
             dma((dp - 1,)), dma((dp - 1,)),
             dma((chunks, dp - 1)), dma((chunks, dp - 1)),
             dma((chunks, bits)), dma((chunks, bits)),

time: 96.8 us -> 93.3 us (0.964)
  Pallas kernels: 91.1 us -> 87.6 us
    pallas_call x1, Pallas kernels: 91.1 us -> 87.6 us  [per_device(): pl.pallas_call(functools.partial(kernel, tm, dp, chunks), out_shape=(jax....]
where the time goes in v3:
time: 93.3 us; the launch traced here: 93.1 us
  Pallas kernels  87.6 us (94%)
  local copies, waits for them, and re-layouts  4.87 us (5%)
    pallas_call x1, Pallas kernels, per_device(): pl.pallas_call(functools.partial(kernel, tm, dp, chunks), out_shape=(jax....  87.6 us
    slice x2, local copies, waits for them, and re-layouts, per_device(): return (dx[None], fin[:, :3 * inner], fin[:, 3 * inner:])  4.17 us

profile of v3, /device:TPU:1, one launch (start us, length us, event | category | flops | bytes accessed | tf_op | source)
XLA Modules:
  0.0 93.1 jit_solution(9348039824027120995)
XLA Ops:
  0.6 87.6 %shard_map.67 = (bf16[128,1024]{1,0:T(8,128)(2,1)}, f32[128,3072]{1,0:T(8,128)}) custom-call(bf16[128,1024]{1,0:T(8,128)(2,1)} %bitcast.4, bf16[128,1024]{1,0:T(8,128)(2,1)} %bitcast.5, bf16[1024,2304]{1,0:T(8,128)(2,1)} %wq_hbm.1, bf16[1024,768]{1,0:T(8,128)(2,1)} %wo_hbm.1), custom_call_target="tpu_custom_call" | custom-call | tf_op jit(solution)/shard_map/pallas_call | solution.py:429
  88.2 0.0 copy-start
  88.2 1.8 %slice.7 = f32[128,768]{1,0:T(8,128)} slice(f32[128,3072]{1,0:T(8,128)} %get-tuple-element.6), slice={[0:128], [2304:3072]} | slice | bytes 786432 | tf_op jit(solution)/shard_map/slice | solution.py:465
  90.0 2.4 %slice.6 = f32[128,2304]{1,0:T(8,128)} slice(f32[128,3072]{1,0:T(8,128)} %get-tuple-element.6), slice={[0:128], [0:2304]} | slice | bytes 2359296 | tf_op jit(solution)/shard_map/slice | solution.py:465
  92.4 0.0 copy-done
  92.4 0.7 copy.8
Async XLA Ops:
  88.2 4.2 %copy-start = (bf16[128,1024]{1,0:T(8,128)(2,1)S(1)}, bf16[128,1024]{1,0:T(8,128)(2,1)}, u32[]{:S(2)}) copy-start(bf16[128,1024]{1,0:T(8,128)(2,1)} %get-tuple-element.5) | copy-start | bytes 786436
